TPU v7x, 32 devices: a whole 2x2x4 slice. The times are simulated.
32 devices in a mesh: groups: 1, wide: 8 (over y, x, core), narrow: 4 (over z).
Axes of the slice: x: 2, y: 2, z: 4, core: 2. Of those that a mesh axis runs over, the one named last changes fastest.
Arguments:
- table_cells: bfloat16 [128, 128, 192], P(('groups', 'wide', 'narrow')), may hold values from -12 to 12
- counts: int32 [128], P(('groups', 'wide', 'narrow')), may hold values from 32 to 128, as said below
- train_count: int32 [1], P('groups'), may hold values from 32 to 96
- norm_gain: float32 [3, 192], replicated, may hold values from 0.5 to 1.5
- feature_in: bfloat16 [192, 576], P('narrow'), may hold values from -0.4375 to 0.4375
- feature_out: bfloat16 [192, 192], P('narrow'), may hold values from -0.4375 to 0.4375
- sample_in: bfloat16 [192, 576], P('narrow'), may hold values from -0.4375 to 0.4375
- sample_out: bfloat16 [192, 192], P('narrow'), may hold values from -0.4375 to 0.4375
- hidden_up: bfloat16 [192, 768], P('narrow'), may hold values from -0.4375 to 0.4375
- hidden_down: bfloat16 [768, 192], P('narrow'), may hold values from -0.21875 to 0.21875
Outputs:
- updated_cells: bfloat16 [128, 128, 192], P(('groups', 'wide', 'narrow'))
Inputs may be any that keep to these rules, and one draw needn't show every extreme that they name: `counts`: feature j of a row is present when j < its count; some row has all 128 features present. Rows 0 to train_count - 1 are the training rows.
All inputs are finite; a program needn't handle non-finite values.
Results may differ from a plain program's by a relative error of at most 0.0086.
Values may be sent and summed in bfloat16 or wider, within the bound.
A program may use at most 64 MiB of HBM per device.

v0:
```python
import jax
import jax.numpy as jnp
from jax import lax
from jax.sharding import PartitionSpec as P

HEADS = 6
epsilon = 1e-05


def normalize(values, gain):
    average = jnp.mean(values, axis=-1, keepdims=True)
    centered = values - average
    spread = jnp.mean(centered * centered, axis=-1, keepdims=True)
    return centered * lax.rsqrt(spread + epsilon) * gain


def attend(packed, valid, head_count):
    length = packed.shape[0]
    model_width = packed.shape[1] // 3
    head_size = model_width // head_count
    scale_factor = 1.0 / jnp.sqrt(jnp.float32(head_size))
    queries = packed[:, :model_width].reshape(length, head_count, head_size)
    key_part = packed[:, model_width : 2 * model_width].reshape(length, head_count, head_size)
    value_part = packed[:, 2 * model_width :].reshape(length, head_count, head_size)
    scores = (
        jnp.einsum("qhd,khd->hqk", queries, key_part, preferred_element_type=jnp.float32)
        * scale_factor
    )
    scores = jnp.where(valid[None, None, :], scores, jnp.float32(-1e30))
    maxima = jnp.max(scores, axis=-1, keepdims=True)
    exponentials = jnp.where(valid[None, None, :], jnp.exp(scores - maxima), jnp.float32(0.0))
    totals = jnp.sum(exponentials, axis=-1, keepdims=True)
    probabilities = (exponentials / totals).astype(jnp.bfloat16)
    context = jnp.einsum(
        "hqk,khd->qhd", probabilities, value_part, preferred_element_type=jnp.float32
    )
    return context.reshape(length, model_width).astype(jnp.bfloat16)


def project(values, weight):
    flat = values.reshape(-1, values.shape[-1])
    return jnp.dot(flat, weight, preferred_element_type=jnp.float32).reshape(
        values.shape[:-1] + (weight.shape[1],)
    )


def body(
    table_cells,
    counts,
    train_count,
    norm_gain,
    feature_in,
    feature_out,
    sample_in,
    sample_out,
    hidden_up,
    hidden_down,
):
    row_local, feats_all, model_width = table_cells.shape
    feat_in_all, feat_out_all = (
        lax.all_gather(feature_in, "narrow", axis=0, tiled=True),
        lax.all_gather(feature_out, "narrow", axis=0, tiled=True),
    )
    feature_ids = jnp.arange(feats_all, dtype=jnp.int32)
    packed = project(table_cells, feat_in_all).astype(jnp.bfloat16)

    def feature_row(pair):
        return attend(pair[0], feature_ids < pair[1], HEADS)

    context = lax.map(feature_row, (packed, counts))
    update = project(context, feat_out_all)
    first = normalize(table_cells.astype(jnp.float32) + update, norm_gain[0]).astype(jnp.bfloat16)
    columns = lax.all_to_all(first, ("wide", "narrow"), split_axis=1, concat_axis=0, tiled=True)
    rows_all, feat_local = (columns.shape[0], columns.shape[1])
    samp_in_all, samp_out_all = (
        lax.all_gather(sample_in, "narrow", axis=0, tiled=True),
        lax.all_gather(sample_out, "narrow", axis=0, tiled=True),
    )
    by_feature = jnp.swapaxes(columns, 0, 1)
    valid = jnp.arange(rows_all, dtype=jnp.int32) < train_count[0]
    packed_samples = project(by_feature, samp_in_all).astype(jnp.bfloat16)
    sample_context = lax.map(lambda column: attend(column, valid, HEADS), packed_samples)
    sample_update = project(sample_context, samp_out_all)
    second = normalize(by_feature.astype(jnp.float32) + sample_update, norm_gain[1]).astype(
        jnp.bfloat16
    )
    up_all, down_all = (
        lax.all_gather(hidden_up, "narrow", axis=0, tiled=True),
        lax.all_gather(hidden_down, "narrow", axis=0, tiled=True),
    )
    hidden = jax.nn.gelu(project(second, up_all), approximate=False).astype(jnp.bfloat16)
    back = project(hidden, down_all)
    result = normalize(second.astype(jnp.float32) + back, norm_gain[2]).astype(jnp.bfloat16)
    result_rows = jnp.swapaxes(result, 0, 1)
    return lax.all_to_all(result_rows, ("wide", "narrow"), split_axis=0, concat_axis=1, tiled=True)


def solution(mesh):
    return jax.shard_map(
        body,
        mesh=mesh,
        in_specs=(
            P(("groups", "wide", "narrow"), None, None),
            P(("groups", "wide", "narrow")),
            P("groups"),
            P(),
            P("narrow", None),
            P("narrow", None),
            P("narrow", None),
            P("narrow", None),
            P("narrow", None),
            P("narrow", None),
        ),
        out_specs=P(("groups", "wide", "narrow"), None, None),
        check_vma=False,
    )
```

profile of v0, /device:TPU:0, one launch (start us, length us, event | category | flops | bytes accessed | tf_op | source)
XLA Modules:
  0.0 134.4 jit_solution(16577640377260590868)
XLA Ops:
  0.0 0.8 fusion.94
  0.8 15.2 %all_gather.19 = bf16[192,192]{1,0:T(8,128)(2,1)S(1)} all-gather(bf16[48,192]{1,0:T(8,128)(2,1)} %param.19), channel_id=1, replica_groups=mesh['groups'=1,'wide'=8,'narrow'=4] {'narrow'}, dimensions={0}, use_global_device_ids=true | all-gather | bytes 92160 | tf_op jit(solution)/shard_map/all_gather | solution.py:62
  16.0 14.4 %all_gather.18 = bf16[192,576]{1,0:T(8,128)(2,1)S(1)} all-gather(bf16[48,576]{1,0:T(8,128)(2,1)} %param.18), channel_id=1, replica_groups=mesh['groups'=1,'wide'=8,'narrow'=4] {'narrow'}, dimensions={0}, use_global_device_ids=true | all-gather | bytes 276480 | tf_op jit(solution)/shard_map/all_gather | solution.py:61
  30.5 1.3 convolution_convert_fusion.3
  31.8 9.3 %while.22 = (s32[]{:T(128)}, bf16[4,128,192]{1,2,0:T(8,128)(2,1)S(1)}, bf16[4,128,576]{1,2,0:T(8,128)(2,1)S(1)}, s32[4]{0:T(128)S(1)}, s32[]{:T(128)}) while((s32[]{:T(128)}, bf16[4,128,192]{1,2,0:T(8,128)(2,1)S(1)}, bf16[4,128,576]{1,2,0:T(8,128)(2,1)S(1)}, s32[4]{0:T(128)S(1)}, s32[]{:T(128)}) %tuple.61), condition=%wide.region_3.4_spmd.clone, body=%wide.region_0.3_spmd.clone.sunk | while | flops 19981440 | bytes 1776221 | solution.py:70
  31.8 0.7 dynamic_slice.20
  32.5 0.7 iota_compare_fusion.4
  34.1 0.7 dynamic_slice.20
  34.8 0.7 iota_compare_fusion.4
  36.5 0.7 dynamic_slice.20
  37.1 0.7 iota_compare_fusion.4
  38.8 0.7 dynamic_slice.20
  39.5 0.7 iota_compare_fusion.4
  41.6 0.9 copy.28
  42.5 5.3 %all-to-all-start = ((bf16[4,128,192]{2,0,1:T(4,128)(2,1)}), bf16[4,128,192]{2,0,1:T(4,128)(2,1)S(1)}, u32[]{:S(2)}, u32[]{:S(2)}) async-start(bf16[4,128,192]{2,0,1:T(4,128)(2,1)} %copy.28), calls=%async_computation | async-start | bytes 524288 | tf_op jit(solution)/shard_map/all_to_all | solution.py:73
  47.8 16.4 %all_gather.21 = bf16[192,192]{1,0:T(8,128)(2,1)S(1)} all-gather(bf16[48,192]{1,0:T(8,128)(2,1)S(1)} %copy-done.4), channel_id=1, replica_groups=mesh['groups'=1,'wide'=8,'narrow'=4] {'narrow'}, dimensions={0}, use_global_device_ids=true | all-gather | bytes 92160 | tf_op jit(solution)/shard_map/all_gather | solution.py:77
  64.3 13.8 %all_gather.20 = bf16[192,576]{1,0:T(8,128)(2,1)S(1)} all-gather(bf16[48,576]{1,0:T(8,128)(2,1)S(1)} %copy-done.3), channel_id=1, replica_groups=mesh['groups'=1,'wide'=8,'narrow'=4] {'narrow'}, dimensions={0}, use_global_device_ids=true | all-gather | bytes 276480 | tf_op jit(solution)/shard_map/all_gather | solution.py:76
  78.1 14.3 %all_gather.22 = bf16[192,768]{1,0:T(8,128)(2,1)S(1)} all-gather(bf16[48,768]{1,0:T(8,128)(2,1)S(1)} %copy-done.2), channel_id=1, replica_groups=mesh['groups'=1,'wide'=8,'narrow'=4] {'narrow'}, dimensions={0}, use_global_device_ids=true | all-gather | bytes 368640 | tf_op jit(solution)/shard_map/all_gather | solution.py:88
  92.3 14.2 %all_gather.23 = bf16[768,192]{1,0:T(8,128)(2,1)S(1)} all-gather(bf16[192,192]{1,0:T(8,128)(2,1)S(1)} %copy-done.1), channel_id=1, replica_groups=mesh['groups'=1,'wide'=8,'narrow'=4] {'narrow'}, dimensions={0}, use_global_device_ids=true | all-gather | bytes 368640 | tf_op jit(solution)/shard_map/all_gather | solution.py:89
  107.3 6.4 %while.23 = (s32[]{:T(128)}, bf16[4,128,192]{1,2,0:T(8,128)(2,1)S(1)}, bf16[4,128,576]{1,2,0:T(8,128)(2,1)S(1)}, s32[]{:T(128)}, s32[]{:T(128)}) while((s32[]{:T(128)}, bf16[4,128,192]{1,2,0:T(8,128)(2,1)S(1)}, bf16[4,128,576]{1,2,0:T(8,128)(2,1)S(1)}, s32[]{:T(128)}, s32[]{:T(128)}) %tuple.58), condition=%wide.region_9.10_spmd.clone, body=%wide.region_6.9_spmd.clone.sunk | while | flops 19981440 | bytes 1776209 | solution.py:82
  114.2 0.8 fusion.43
  115.0 3.8 %fusion.46 = (f32[4,128]{1,0:T(4,128)S(1)}, f32[4,128,192]{1,2,0:T(8,128)S(1)}) fusion(bf16[4,128,192]{1,2,0:T(8,128)(2,1)S(1)} %multiply_convert_fusion, bf16[768,192]{1,0:T(8,128)(2,1)S(1)} %all_gather.23, f32[4,128,768]{2,1,0:T(8,128)S(1)} %get-tuple-element.114, u8[128,768]{1,0:T(8,128)(4,1)S(1)} %get-tuple-element.78, ...), kind=kOutput, calls=%fused_computation.80 | convolution fusion | flops 178814464 | bytes 2656256 | tf_op jit(solution)/shard_map/dot_general | solution.py:42
  119.2 14.2 %all_to_all.36 = bf16[128,4,192]{2,1,0:T(4,128)(2,1)S(1)} all-to-all(bf16[128,4,192]{2,1,0:T(4,128)(2,1)S(1)} %copy.33), channel_id=1, replica_groups=mesh['groups'=1,'wide'=8,'narrow'=4] {'wide','narrow'}, dimensions={0} | all-to-all | bytes 393216 | tf_op jit(solution)/shard_map/all_to_all | solution.py:95
  133.6 0.9 copy.35
  (86 shorter events, 12.1 us)
Async XLA Ops:
  0.0 31.8 %copy-start.5 = (s32[4]{0:T(128)S(1)}, s32[4]{0:T(128)}, u32[]{:S(2)}) copy-start(s32[4]{0:T(128)} %param.15) | copy-start | bytes 52
  31.8 9.3 %copy-start = (bf16[4,128,192]{1,2,0:T(8,128)(2,1)S(1)}, bf16[4,128,192]{1,2,0:T(8,128)(2,1)}, u32[]{:S(2)}) copy-start(bf16[4,128,192]{1,2,0:T(8,128)(2,1)} %param.14) | copy-start | bytes 589828
  41.1 6.7 %copy-start.4 = (bf16[48,192]{1,0:T(8,128)(2,1)S(1)}, bf16[48,192]{1,0:T(8,128)(2,1)}, u32[]{:S(2)}) copy-start(bf16[48,192]{1,0:T(8,128)(2,1)} %param.21) | copy-start | bytes 55300
  41.1 23.2 %copy-start.3 = (bf16[48,576]{1,0:T(8,128)(2,1)S(1)}, bf16[48,576]{1,0:T(8,128)(2,1)}, u32[]{:S(2)}) copy-start(bf16[48,576]{1,0:T(8,128)(2,1)} %param.20) | copy-start | bytes 165892
  41.1 36.9 %copy-start.2 = (bf16[48,768]{1,0:T(8,128)(2,1)S(1)}, bf16[48,768]{1,0:T(8,128)(2,1)}, u32[]{:S(2)}) copy-start(bf16[48,768]{1,0:T(8,128)(2,1)} %param.22) | copy-start | bytes 221188
  41.4 50.9 %copy-start.1 = (bf16[192,192]{1,0:T(8,128)(2,1)S(1)}, bf16[192,192]{1,0:T(8,128)(2,1)}, u32[]{:S(2)}) copy-start(bf16[192,192]{1,0:T(8,128)(2,1)} %param.23) | copy-start | bytes 221188
  42.5 64.1 %all-to-all-start = ((bf16[4,128,192]{2,0,1:T(4,128)(2,1)}), bf16[4,128,192]{2,0,1:T(4,128)(2,1)S(1)}, u32[]{:S(2)}, u32[]{:S(2)}) async-start(bf16[4,128,192]{2,0,1:T(4,128)(2,1)} %copy.28), calls=%async_computation | async-start | bytes 524288 | tf_op jit(solution)/shard_map/all_to_all | solution.py:73
where the time goes:
time: 135 us; the launch traced here: 134 us
  blocking collectives  103 us (76%)
  matrix products  13.6 us (10%)
  local copies, waits for them, and re-layouts  6.32 us (5%)
  other arithmetic  5.99 us (4%)
  starting transfers between devices  5.33 us (4%)
    all_gather x1, blocking collectives, body(): lax.all_gather(sample_out, 'narrow', axis=0, tiled=True)  16.4 us
    all_gather x1, blocking collectives, body(): lax.all_gather(feature_out, 'narrow', axis=0, tiled=True)  15.2 us
    all_gather x1, blocking collectives, body(): lax.all_gather(feature_in, 'narrow', axis=0, tiled=True)  14.4 us
    all_gather x1, blocking collectives, body(): lax.all_gather(hidden_up, 'narrow', axis=0, tiled=True)  14.3 us
    all_to_all x1, blocking collectives, body(): lax.all_to_all(result_rows, ('wide', 'narrow'), split_axis=0, concat_axis...  14.2 us
    all_gather x1, blocking collectives, body(): lax.all_gather(hidden_down, 'narrow', axis=0, tiled=True)  14.2 us
    all_gather x1, blocking collectives, body(): lax.all_gather(sample_in, 'narrow', axis=0, tiled=True)  13.8 us
    dot_general x6, matrix products, project(): jnp.dot(flat, weight, preferred_element_type=jnp.float32)  6.72 us
  transfers between devices with their start and end apart: 1, of which 0 were waited for; matrix products, arithmetic and copies ran while one was open for 0% of the time, Pallas kernels for 0%

commit v1 on v0

--- a/solution.py
+++ b/solution.py
@@ -1,3 +1,4 @@
+import functools
 import jax
 import jax.numpy as jnp
 from jax import lax
@@ -5,6 +6,39 @@
 
 HEADS = 6
 epsilon = 1e-05
+
+
+def save_words_now(xs, on_dim):
+    xs = jnp.moveaxis(xs, 0, on_dim)
+    out_arr = xs.shape
+    later = xs.reshape(
+        *out_arr[:on_dim], out_arr[on_dim] * out_arr[on_dim + 1], *out_arr[on_dim + 2 :]
+    )
+    return later
+
+
+def _view_values(local, device_axis):
+    world_n = lax.axis_size(device_axis)
+    formed = local[None]
+    for idx in range(world_n.bit_length() - 1):
+        step_out = 1 << idx
+        reached = lax.ppermute(
+            formed, axis_name=device_axis, perm=[(t, t ^ step_out) for t in range(world_n)]
+        )
+        z1 = jnp.stack([formed, reached])
+        w_next = lax.axis_index(device_axis)
+        z = w_next >> idx & 1
+        formed = jnp.where(z == 0, z1, z1[::-1]).reshape(-1, *local.shape)
+    return formed
+
+
+def recast_the_sites(local_array, slab_in, dimension_no):
+    local_next = _view_values(local_array, slab_in)
+    parts_out = save_words_now(local_next, dimension_no)
+    return parts_out
+
+
+_fit_sample = functools.partial(recast_the_sites, slab_in="narrow", dimension_no=0)
 
 
 def normalize(values, gain):
@@ -74,7 +108,7 @@
     rows_all, feat_local = (columns.shape[0], columns.shape[1])
     samp_in_all, samp_out_all = (
         lax.all_gather(sample_in, "narrow", axis=0, tiled=True),
-        lax.all_gather(sample_out, "narrow", axis=0, tiled=True),
+        _fit_sample(sample_out),
     )
     by_feature = jnp.swapaxes(columns, 0, 1)
     valid = jnp.arange(rows_all, dtype=jnp.int32) < train_count[0]

time: 135 us -> 124 us (0.919)
  blocking collectives: 103 us -> 88.5 us
  starting transfers between devices: 5.33 us -> 8.71 us
    all_gather x1 -> x0, blocking collectives: 16.4 us -> none  [body(): lax.all_gather(sample_out, 'narrow', axis=0, tiled=True)]
    all_gather x1, blocking collectives: 14.3 us -> 18.1 us  [body(): lax.all_gather(hidden_up, 'narrow', axis=0, tiled=True)]
    ppermute x0 -> x2, starting transfers between devices: none -> 3.78 us  [_view_values(): lax.ppermute(formed, axis_name=device_axis, perm=[(t, t ^ step_out) for t...]
    all_gather x1, blocking collectives: 15.2 us -> 13.7 us  [body(): lax.all_gather(feature_out, 'narrow', axis=0, tiled=True)]
  transfers between devices with their start and end apart: 1 -> 3, of which waited for: 0 -> 0; matrix products, arithmetic and copies ran while one was open for 0% -> 10% of each run, Pallas kernels for 0% -> 0%
where the time goes in v1:
time: 124 us
  blocking collectives  88.5 us (71%)
  matrix products  13.6 us (11%)
  starting transfers between devices  8.71 us (7%)
  local copies, waits for them, and re-layouts  6.32 us (5%)
  other arithmetic  6.07 us (5%)
    all_gather x1, blocking collectives, body(): lax.all_gather(hidden_up, 'narrow', axis=0, tiled=True)  18.1 us
    all_to_all x1, blocking collectives, body(): lax.all_to_all(result_rows, ('wide', 'narrow'), split_axis=0, concat_axis...  14.6 us
    all_gather x1, blocking collectives, body(): lax.all_gather(hidden_down, 'narrow', axis=0, tiled=True)  14.2 us
    all_gather x1, blocking collectives, body(): lax.all_gather(sample_in, 'narrow', axis=0, tiled=True)  14 us
    all_gather x1, blocking collectives, body(): lax.all_gather(feature_in, 'narrow', axis=0, tiled=True)  13.9 us
    all_gather x1, blocking collectives, body(): lax.all_gather(feature_out, 'narrow', axis=0, tiled=True)  13.7 us
    dot_general x6, matrix products, project(): jnp.dot(flat, weight, preferred_element_type=jnp.float32)  6.72 us
    all_to_all x1, starting transfers between devices, body(): lax.all_to_all(first, ('wide', 'narrow'), split_axis=1, concat_axis=0, ti...  4.93 us
  transfers between devices with their start and end apart: 3, of which 0 were waited for; matrix products, arithmetic and copies ran while one was open for 10% of the time, Pallas kernels for 0%

profile of v1, /device:TPU:0, one launch (start us, length us, event | category | flops | bytes accessed | tf_op | source)
XLA Modules:
  0.0 123.9 jit_solution(10382979827139180458)
XLA Ops:
  0.0 3.0 %collective-permute-start = (bf16[1,48,192]{2,1,0:T(8,128)(2,1)}, bf16[1,48,192]{2,1,0:T(8,128)(2,1)S(1)}, u32[]{:S(2)}, u32[]{:S(2)}) collective-permute-start(bf16[1,48,192]{2,1,0:T(8,128)(2,1)} %bitcast.182), channel_id=1, source_target_pairs={{0,1},{1,0},{2,3},{3,2},{4,5},{5,4},{6,7},{7,6},{8,9},{9,8},{10,11... | collective-permute-start | bytes 55304 | tf_op jit(solution)/shard_map/ppermute | solution.py:25
  3.0 0.8 fusion.94
  3.8 13.7 %all_gather.16 = bf16[192,192]{1,0:T(8,128)(2,1)S(1)} all-gather(bf16[48,192]{1,0:T(8,128)(2,1)} %param.19), channel_id=1, replica_groups=mesh['groups'=1,'wide'=8,'narrow'=4] {'narrow'}, dimensions={0}, use_global_device_ids=true | all-gather | bytes 92160 | tf_op jit(solution)/shard_map/all_gather | solution.py:96
  17.5 13.9 %all_gather.15 = bf16[192,576]{1,0:T(8,128)(2,1)S(1)} all-gather(bf16[48,576]{1,0:T(8,128)(2,1)} %param.18), channel_id=1, replica_groups=mesh['groups'=1,'wide'=8,'narrow'=4] {'narrow'}, dimensions={0}, use_global_device_ids=true | all-gather | bytes 276480 | tf_op jit(solution)/shard_map/all_gather | solution.py:95
  31.4 1.3 %convolution_convert_fusion.3 = bf16[4,128,576]{1,2,0:T(8,128)(2,1)S(1)} fusion(bf16[4,128,192]{1,2,0:T(8,128)(2,1)} %param.14, bf16[192,576]{1,0:T(8,128)(2,1)S(1)} %all_gather.15), kind=kOutput, calls=%fused_computation.55 | convolution fusion | flops 113541120 | bytes 1007616 | tf_op jit(solution)/shard_map/dot_general | solution.py:76
  32.8 9.3 %while.22 = (s32[]{:T(128)}, bf16[4,128,192]{1,2,0:T(8,128)(2,1)S(1)}, bf16[4,128,576]{1,2,0:T(8,128)(2,1)S(1)}, s32[4]{0:T(128)S(1)}, s32[]{:T(128)}) while((s32[]{:T(128)}, bf16[4,128,192]{1,2,0:T(8,128)(2,1)S(1)}, bf16[4,128,576]{1,2,0:T(8,128)(2,1)S(1)}, s32[4]{0:T(128)S(1)}, s32[]{:T(128)}) %tuple.62), condition=%wide.region_3.4_spmd.clone, body=%wide.region_0.3_spmd.clone.sunk | while | flops 19981440 | bytes 1776221 | solution.py:104
  32.8 0.7 dynamic_slice.20
  33.5 0.7 iota_compare_fusion.4
  35.1 0.7 dynamic_slice.20
  35.8 0.7 iota_compare_fusion.4
  37.4 0.7 dynamic_slice.20
  38.1 0.7 iota_compare_fusion.4
  40.4 0.7 iota_compare_fusion.4
  42.6 0.9 copy.30
  43.5 4.9 %all-to-all-start = ((bf16[4,128,192]{2,0,1:T(4,128)(2,1)}), bf16[4,128,192]{2,0,1:T(4,128)(2,1)S(1)}, u32[]{:S(2)}, u32[]{:S(2)}) async-start(bf16[4,128,192]{2,0,1:T(4,128)(2,1)} %copy.30), calls=%async_computation | async-start | bytes 524288 | tf_op jit(solution)/shard_map/all_to_all | solution.py:107
  48.4 18.1 %all_gather.18 = bf16[192,768]{1,0:T(8,128)(2,1)S(1)} all-gather(bf16[48,768]{1,0:T(8,128)(2,1)S(1)} %copy-done.2), channel_id=1, replica_groups=mesh['groups'=1,'wide'=8,'narrow'=4] {'narrow'}, dimensions={0}, use_global_device_ids=true | all-gather | bytes 368640 | tf_op jit(solution)/shard_map/all_gather | solution.py:122
  66.5 14.2 %all_gather.19 = bf16[768,192]{1,0:T(8,128)(2,1)S(1)} all-gather(bf16[192,192]{1,0:T(8,128)(2,1)S(1)} %copy-done.1), channel_id=1, replica_groups=mesh['groups'=1,'wide'=8,'narrow'=4] {'narrow'}, dimensions={0}, use_global_device_ids=true | all-gather | bytes 368640 | tf_op jit(solution)/shard_map/all_gather | solution.py:123
  80.7 0.8 collective-permute-start.1
  81.5 14.0 %all_gather.17 = bf16[192,576]{1,0:T(8,128)(2,1)S(1)} all-gather(bf16[48,576]{1,0:T(8,128)(2,1)S(1)} %copy-done.3), channel_id=1, replica_groups=mesh['groups'=1,'wide'=8,'narrow'=4] {'narrow'}, dimensions={0}, use_global_device_ids=true | all-gather | bytes 276480 | tf_op jit(solution)/shard_map/all_gather | solution.py:110
  96.4 6.4 %while.23 = (s32[]{:T(128)}, bf16[4,128,192]{1,2,0:T(8,128)(2,1)S(1)}, bf16[4,128,576]{1,2,0:T(8,128)(2,1)S(1)}, s32[]{:T(128)}, s32[]{:T(128)}) while((s32[]{:T(128)}, bf16[4,128,192]{1,2,0:T(8,128)(2,1)S(1)}, bf16[4,128,576]{1,2,0:T(8,128)(2,1)S(1)}, s32[]{:T(128)}, s32[]{:T(128)}) %tuple.59), condition=%wide.region_9.10_spmd.clone, body=%wide.region_6.9_spmd.clone.sunk | while | flops 19981440 | bytes 1776209 | solution.py:116
  103.3 0.8 fusion.43
  104.1 3.8 %fusion.46 = (f32[4,128]{1,0:T(4,128)S(1)}, f32[4,128,192]{1,2,0:T(8,128)S(1)}) fusion(bf16[4,128,192]{1,2,0:T(8,128)(2,1)S(1)} %multiply_convert_fusion, bf16[768,192]{1,0:T(8,128)(2,1)S(1)} %all_gather.19, f32[4,128,768]{2,1,0:T(8,128)S(1)} %get-tuple-element.116, u8[128,768]{1,0:T(8,128)(4,1)S(1)} %get-tuple-element.78, ...), kind=kOutput, calls=%fused_computation.80 | convolution fusion | flops 178814464 | bytes 2656256 | tf_op jit(solution)/shard_map/dot_general | solution.py:76
  108.3 14.6 %all_to_all.36 = bf16[128,4,192]{2,1,0:T(4,128)(2,1)S(1)} all-to-all(bf16[128,4,192]{2,1,0:T(4,128)(2,1)S(1)} %copy.36), channel_id=1, replica_groups=mesh['groups'=1,'wide'=8,'narrow'=4] {'wide','narrow'}, dimensions={0} | all-to-all | bytes 393216 | tf_op jit(solution)/shard_map/all_to_all | solution.py:129
  123.0 0.9 copy.38
  (93 shorter events, 12.8 us)
Async XLA Ops:
  0.0 32.8 %copy-start.5 = (s32[4]{0:T(128)S(1)}, s32[4]{0:T(128)}, u32[]{:S(2)}) copy-start(s32[4]{0:T(128)} %param.15) | copy-start | bytes 52
  0.0 80.7 %collective-permute-start = (bf16[1,48,192]{2,1,0:T(8,128)(2,1)}, bf16[1,48,192]{2,1,0:T(8,128)(2,1)S(1)}, u32[]{:S(2)}, u32[]{:S(2)}) collective-permute-start(bf16[1,48,192]{2,1,0:T(8,128)(2,1)} %bitcast.182), channel_id=1, source_target_pairs={{0,1},{1,0},{2,3},{3,2},{4,5},{5,4},{6,7},{7,6},{8,9},{9,8},{10,11... | collective-permute-start | bytes 55304 | tf_op jit(solution)/shard_map/ppermute | solution.py:25
  32.8 9.3 %copy-start = (bf16[4,128,192]{1,2,0:T(8,128)(2,1)S(1)}, bf16[4,128,192]{1,2,0:T(8,128)(2,1)}, u32[]{:S(2)}) copy-start(bf16[4,128,192]{1,2,0:T(8,128)(2,1)} %param.14) | copy-start | bytes 589828
  42.1 6.3 %copy-start.2 = (bf16[48,768]{1,0:T(8,128)(2,1)S(1)}, bf16[48,768]{1,0:T(8,128)(2,1)}, u32[]{:S(2)}) copy-start(bf16[48,768]{1,0:T(8,128)(2,1)} %param.22) | copy-start | bytes 221188
  42.1 24.4 %copy-start.1 = (bf16[192,192]{1,0:T(8,128)(2,1)S(1)}, bf16[192,192]{1,0:T(8,128)(2,1)}, u32[]{:S(2)}) copy-start(bf16[192,192]{1,0:T(8,128)(2,1)} %param.23) | copy-start | bytes 221188
  42.4 38.3 %copy-start.4 = (bf16[48,192]{1,0:T(8,128)(2,1)S(1)}, bf16[48,192]{1,0:T(8,128)(2,1)}, u32[]{:S(2)}) copy-start(bf16[48,192]{1,0:T(8,128)(2,1)} %param.21) | copy-start | bytes 55300
  42.4 39.1 %copy-start.3 = (bf16[48,576]{1,0:T(8,128)(2,1)S(1)}, bf16[48,576]{1,0:T(8,128)(2,1)}, u32[]{:S(2)}) copy-start(bf16[48,576]{1,0:T(8,128)(2,1)} %param.20) | copy-start | bytes 165892
  43.5 52.1 %all-to-all-start = ((bf16[4,128,192]{2,0,1:T(4,128)(2,1)}), bf16[4,128,192]{2,0,1:T(4,128)(2,1)S(1)}, u32[]{:S(2)}, u32[]{:S(2)}) async-start(bf16[4,128,192]{2,0,1:T(4,128)(2,1)} %copy.30), calls=%async_computation | async-start | bytes 524288 | tf_op jit(solution)/shard_map/all_to_all | solution.py:107
  80.7 14.8 %collective-permute-start.1 = (bf16[2,48,192]{2,1,0:T(8,128)(2,1)S(1)}, bf16[2,48,192]{2,1,0:T(8,128)(2,1)S(1)}, u32[]{:S(2)}, u32[]{:S(2)}) collective-permute-start(bf16[2,48,192]{2,1,0:T(8,128)(2,1)S(1)} %get-tuple-element.102), channel_id=1, source_target_pairs={{0,2},{1,3},{2,0},{3,1},{4,6},{5,7},{6,4},{7,5},{8,10},{9,11},{10,... | collective-permute-start | bytes 110600 | tf_op jit(solution)/shard_map/ppermute | solution.py:25
